TPU v7x, 32 devices: a whole 2x2x4 slice. The times are simulated.
32 devices in a mesh: groups: 2 (over y), chan: 4 (over z), space: 2 (over x), pair: 2 (over core).
Axes of the slice: x: 2, y: 2, z: 4, core: 2. Of those that a mesh axis runs over, the one named last changes fastest.
Arguments:
- grad_out: bfloat16 [512, 32, 1024], P('chan', ('groups', 'space', 'pair')), parts along dimension 1, may hold values from -6 to 6
- conv_weight: bfloat16 [27, 512, 512], P(None, 'chan'), may hold values from -0.0546875 to 0.0546875
- pre_act: bfloat16 [32, 1024, 512], P(('groups', 'space', 'pair'), 'chan'), parts along dimension 0, may hold values from -6 to 6
- down_weight: bfloat16 [8, 256, 512], replicated, may hold values from -0.25 to 0.25
Outputs:
- grad_fine: bfloat16 [32, 1024, 8, 256], P(('groups', 'space', 'pair'), 'chan'), parts along dimension 0
There are 2 independent parts, one for each index of `groups`. A program takes and returns all parts, laid end to end along the dimension named above; an argument that names none is the same for every part. Nothing has to cross between parts.
All inputs are finite; a program needn't handle non-finite values.
Results may differ from a plain program's by a relative error of at most 0.025.
Values may be sent and summed in bfloat16 or wider, within the bound.
No kernel may reach another device: no remote copies, remote signals or barrier semaphores. Data moves between devices by JAX's collectives and lax.ppermute only.
A program may use at most 64 MiB of HBM per device.

v0:
```python
import math
import jax
import jax.numpy as jnp
from jax import lax
from jax.sharding import PartitionSpec as P

NZ = 8


def with_halo(cells, sides, width):
    for axis, dim in sides:
        count = lax.axis_size(axis)
        ends = count - 1
        head = lax.slice_in_dim(cells, 0, width, axis=dim)
        tail = lax.slice_in_dim(cells, cells.shape[dim] - width, cells.shape[dim], axis=dim)
        cells = jnp.concatenate(
            [
                lax.ppermute(tail, axis, [(i, (i + 1) % count) for i in range(ends)]),
                cells,
                lax.ppermute(head, axis, [((i + 1) % count, i) for i in range(ends)]),
            ],
            axis=dim,
        )
    return cells


def shifted_stack(padded, depth):
    extent = padded.shape[1] - 2
    plane_len = padded.shape[2]
    widened = jnp.pad(padded, ((0, 0), (0, 0), (depth + 1, depth + 1)))
    z_index = jnp.arange(plane_len, dtype=jnp.int32) % depth
    pieces = []
    for step_x in (-1, 0, 1):
        x_rows = widened[:, 1 - step_x : 1 - step_x + extent, :]
        for step_y in (-1, 0, 1):
            for step_z in (-1, 0, 1):
                offset = step_y * depth + step_z
                piece = x_rows[:, :, depth + 1 - offset : depth + 1 - offset + plane_len]
                inside = (z_index - step_z >= 0) & (z_index - step_z < depth)
                pieces.append(jnp.where(inside, piece, jnp.zeros_like(piece)))
    return jnp.stack(pieces)


def gelu_slope(values):
    return 0.5 * (1.0 + jax.scipy.special.erf(values / math.sqrt(2.0))) + values * jnp.exp(
        -0.5 * values * values
    ) / math.sqrt(2.0 * math.pi)


def body(grad_out, conv_weight, pre_act, down_weight):
    padded = with_halo(grad_out, ((("space", "pair"), 1),), 1)
    stacked = shifted_stack(padded, NZ)
    partial_sum = lax.dot_general(
        stacked, conv_weight, (((0, 1), (0, 1)), ((), ())), preferred_element_type=jnp.float32
    )
    owned = lax.psum_scatter(
        partial_sum.astype(jnp.bfloat16), "chan", scatter_dimension=2, tiled=True
    )
    grad_act = lax.all_to_all(owned, "chan", split_axis=1, concat_axis=2, tiled=True)
    values = pre_act.astype(jnp.float32)
    grad_pre = (grad_act.astype(jnp.float32) * gelu_slope(values)).astype(jnp.bfloat16)
    result = lax.dot_general(
        grad_pre, down_weight, (((2,), (2,)), ((), ())), preferred_element_type=jnp.float32
    )
    return result.astype(jnp.bfloat16)


def solution(mesh):
    in_specs = (
        P("chan", ("groups", "space", "pair"), None),
        P(None, "chan", None),
        P(("groups", "space", "pair"), "chan", None),
        P(),
    )
    out_specs = P(("groups", "space", "pair"), "chan", None, None)
    return jax.shard_map(body, mesh=mesh, in_specs=in_specs, out_specs=out_specs, check_vma=False)
```

profile of v0, /device:TPU:0, one launch (start us, length us, event | category | flops | bytes accessed | tf_op | source)
XLA Modules:
  0.0 204.0 jit_solution(13061538225299000226)
XLA Ops:
  6.5 2.8 %copy.39 = bf16[128,4,1024]{0,2,1:T(8,128)(2,1)} copy(bf16[128,4,1024]{2,1,0:T(4,128)(2,1)} %param.4) | data formatting | bytes 2097152 | tf_op args[0]
  9.3 1.2 fusion.98
  10.5 2.4 %collective-permute-start = (bf16[128,1,1024]{0,2,1:T(8,128)(2,1)S(1)}, bf16[128,1,1024]{0,2,1:T(8,128)(2,1)S(1)}, u32[]{:S(2)}, u32[]{:S(2)}) collective-permute-start(bf16[128,1,1024]{0,2,1:T(8,128)(2,1)S(1)} %get-tuple-element.5), channel_id=1, source_target_pairs={{0,1},{1,2},{2,3},{4,5},{5,6},{6,7},{8,9},{9,10},{10,11},{12,13},{... | collective-permute-start | bytes 786440 | tf_op jit(solution)/shard_map/ppermute | solution.py:18
  12.9 1.3 collective-permute-start.1
  14.2 4.2 %collective-permute-done.1 = bf16[128,1,1024]{0,2,1:T(8,128)(2,1)S(1)} collective-permute-done((bf16[128,1,1024]{0,2,1:T(8,128)(2,1)S(1)}, bf16[128,1,1024]{0,2,1:T(8,128)(2,1)S(1)}, u32[]{:S(2)}, u32[]{:S(2)}) %collective-permute-start.1) | collective-permute-done | bytes 262176 | tf_op jit(solution)/shard_map/ppermute | solution.py:20
  18.4 1.6 fusion.18
  23.1 0.6 fusion.59
  23.7 0.6 fusion.57
  24.8 0.6 fusion.53
  25.4 0.6 fusion.51
  29.8 0.6 fusion.37
  30.4 0.6 fusion.35
  33.1 0.8 fusion.24
  35.0 17.0 %bitcast_convert_fusion = bf16[4,1024,512]{2,1,0:T(8,128)(2,1)} fusion(bf16[27,128,4,1024]{1,3,0,2:T(8,128)(2,1)S(1)} %fusion.20, bf16[27,128,512]{2,1,0:T(8,128)(2,1)S(1)} %copy-done), kind=kOutput, calls=%fused_computation | convolution fusion | flops 14497611776 | bytes 36044800 | tf_op jit(solution)/shard_map/dot_general | solution.py:53
  52.0 8.0 %copy.76 = bf16[4,1024,512]{1,0,2:T(4,128)(2,1)} copy(bf16[4,1024,512]{2,1,0:T(8,128)(2,1)} %bitcast_convert_fusion) | data formatting | bytes 8388608
  60.0 6.5 %copy.79 = bf16[64,8,4,1024]{3,1,2,0:T(8,128)(2,1)} copy(bf16[64,8,4,1024]{3,2,1,0:T(4,128)(2,1)} %bitcast.184) | data formatting | bytes 8388608
  66.5 81.7 %reduce-scatter.4.cloned.1.call-done = bf16[128,4096]{1,0:T(8,128)(2,1)} async-done(((bf16[512,4096]{1,0:T(8,128)(2,1)}), bf16[128,4096]{1,0:T(8,128)(2,1)}) %reduce-scatter.4.cloned.1.call-update) | async-done | bytes 1048592
  148.2 1.8 reshape.11
  150.0 1.5 copy.71
  151.5 29.8 %all_to_all.4 = bf16[4,1024,128]{2,0,1:T(4,128)(2,1)S(1)} all-to-all(bf16[4,1024,128]{2,0,1:T(4,128)(2,1)S(1)} %copy.71), channel_id=1, replica_groups=mesh['groups'=2,'chan'=4,'space'=2,'pair'=2] {'chan'}, dimensions={1} | all-to-all | bytes 2097152 | tf_op jit(solution)/shard_map/all_to_all | solution.py:59
  181.4 2.7 %copy.72 = f32[4,256,4,128]{3,2,1,0:T(4,128)} copy(f32[4,256,4,128]{3,0,1,2:T(4,128)S(1)} %convert_bitcast_fusion) | data formatting | bytes 4194304 | tf_op jit(solution)/shard_map/convert_element_type | solution.py:61
  184.1 3.3 %reshape.4 = f32[4,256,512]{2,1,0:T(8,128)} reshape(f32[4,256,4,128]{3,2,1,0:T(4,128)} %copy.72) | data formatting | bytes 4194304 | tf_op jit(solution)/shard_map/convert_element_type | solution.py:61
  187.4 5.3 %convolution_convert_fusion = bf16[4,256,8,256]{3,1,2,0:T(8,128)(2,1)S(1)} fusion(bf16[8,256,512]{2,1,0:T(8,128)(2,1)} %param.7, f32[4,256,512]{2,1,0:T(8,128)} %reshape.4, bf16[4,256,512]{2,1,0:T(8,128)(2,1)} %param.6), kind=kOutput, calls=%fused_computation.10 | convolution fusion | flops 2155347968 | bytes 9437184 | tf_op jit(solution)/shard_map/dot_general | solution.py:62
  192.7 4.5 %copy.73 = bf16[4,256,8,256]{3,2,1,0:T(8,128)(2,1)} copy(bf16[4,256,8,256]{3,1,2,0:T(8,128)(2,1)S(1)} %convolution_convert_fusion) | data formatting | bytes 8388608 | tf_op jit(solution)/shard_map/convert_element_type | solution.py:65
  (33 shorter events, 10.5 us)
Async XLA Ops:
  6.5 28.4 %copy-start = (bf16[27,128,512]{2,1,0:T(8,128)(2,1)S(1)}, bf16[27,128,512]{2,1,0:T(8,128)(2,1)}, u32[]{:S(2)}) copy-start(bf16[27,128,512]{2,1,0:T(8,128)(2,1)} %param.5) | copy-start | bytes 10616836
  6.5 141.6 %reduce-scatter.4.cloned.1.call-start = ((), (), s32[]{:S(2)}) async-start(), calls=%async_computation.2 | async-start | bytes 5242880
  9.3 12.8 %copy-start.2 = (bf16[128,4,1024]{0,2,1:T(8,128)(2,1)S(1)}, bf16[128,4,1024]{0,2,1:T(8,128)(2,1)}, u32[]{:S(2)}) copy-start(bf16[128,4,1024]{0,2,1:T(8,128)(2,1)} %copy.39) | copy-start | bytes 3145732
  10.5 3.7 %collective-permute-start = (bf16[128,1,1024]{0,2,1:T(8,128)(2,1)S(1)}, bf16[128,1,1024]{0,2,1:T(8,128)(2,1)S(1)}, u32[]{:S(2)}, u32[]{:S(2)}) collective-permute-start(bf16[128,1,1024]{0,2,1:T(8,128)(2,1)S(1)} %get-tuple-element.5), channel_id=1, source_target_pairs={{0,1},{1,2},{2,3},{4,5},{5,6},{6,7},{8,9},{9,10},{10,11},{12,13},{... | collective-permute-start | bytes 786440 | tf_op jit(solution)/shard_map/ppermute | solution.py:18
  12.9 5.5 %collective-permute-start.1 = (bf16[128,1,1024]{0,2,1:T(8,128)(2,1)S(1)}, bf16[128,1,1024]{0,2,1:T(8,128)(2,1)S(1)}, u32[]{:S(2)}, u32[]{:S(2)}) collective-permute-start(bf16[128,1,1024]{0,2,1:T(8,128)(2,1)S(1)} %get-tuple-element.6), channel_id=1, source_target_pairs={{1,0},{2,1},{3,2},{5,4},{6,5},{7,6},{9,8},{10,9},{11,10},{13,12},{... | collective-permute-start | bytes 786440 | tf_op jit(solution)/shard_map/ppermute | solution.py:20
  184.1 13.1 %copy-start.1 = (bf16[27,128,512]{2,1,0:T(8,128)(2,1)S(1)}, bf16[27,128,512]{2,1,0:T(8,128)(2,1)}, u32[]{:S(2)}) copy-start(bf16[27,128,512]{2,1,0:T(8,128)(2,1)} %param.5) | copy-start | bytes 10616836
Sparse Core Ops, SparseCore 0:
  66.6 81.4 reduce-scatter.3
where the time goes:
time: 204 us
  waiting for transfers between devices  85.8 us (42%)
  local copies, waits for them, and re-layouts  32.2 us (16%)
  blocking collectives  29.8 us (15%)
  matrix products  22.4 us (11%)
  other arithmetic  16.5 us (8%)
  between operations  13.7 us (7%)
  starting transfers between devices  3.67 us (2%)
    unnamed x2, waiting for transfers between devices  81.7 us
    all_to_all x1, blocking collectives, body(): lax.all_to_all(owned, 'chan', split_axis=1, concat_axis=2, tiled=True)  29.8 us
    unnamed x10, local copies, waits for them, and re-layouts  19.1 us
    dot_general x1, matrix products, body(): lax.dot_general(stacked, conv_weight, (((0, 1), (0, 1)), ((), ())), prefe...  17 us
    unnamed x26, other arithmetic  14.2 us
    convert_element_type x2, local copies, waits for them, and re-layouts, body(): grad_act.astype(jnp.float32) * gelu_slope(values)  5.93 us
    dot_general x1, matrix products, body(): lax.dot_general(grad_pre, down_weight, (((2,), (2,)), ((), ())), preferre...  5.33 us
    convert_element_type x1, local copies, waits for them, and re-layouts, body(): return result.astype(jnp.bfloat16)  4.47 us
  transfers between devices with their start and end apart: 3, of which 2 were waited for; matrix products, arithmetic and copies ran while one was open for 0% of the time, Pallas kernels for 0%

commit v1 on v0

--- a/solution.py
+++ b/solution.py
@@ -5,6 +5,17 @@
 from jax.sharding import PartitionSpec as P
 
 NZ = 8
+
+
+def cut_along(array, dim, size):
+    before, after = (array.shape[:dim], array.shape[dim + 1 :])
+    return jnp.moveaxis(array.reshape(*before, size, -1, *after), dim, 0)
+
+
+def laid_out(blocks, dim):
+    blocks = jnp.moveaxis(blocks, 0, dim)
+    shape = blocks.shape
+    return blocks.reshape(*shape[:dim], shape[dim] * shape[dim + 1], *shape[dim + 2 :])
 
 
 def with_halo(cells, sides, width):
@@ -56,7 +67,14 @@
     owned = lax.psum_scatter(
         partial_sum.astype(jnp.bfloat16), "chan", scatter_dimension=2, tiled=True
     )
-    grad_act = lax.all_to_all(owned, "chan", split_axis=1, concat_axis=2, tiled=True)
+    size, place = (lax.axis_size("chan"), lax.axis_index("chan"))
+    pieces_2 = cut_along(owned, 1, size)
+    finished = [pieces_2[place]]
+    for lap in range(1, size):
+        sent = pieces_2[place ^ lap]
+        finished.append(lax.ppermute(sent, "chan", [(i_2, i_2 ^ lap) for i_2 in range(size)]))
+    pieces_2 = jnp.stack(finished)[place ^ jnp.arange(size)]
+    grad_act = laid_out(pieces_2, 2)
     values = pre_act.astype(jnp.float32)
     grad_pre = (grad_act.astype(jnp.float32) * gelu_slope(values)).astype(jnp.bfloat16)
     result = lax.dot_general(

time: 204 us -> 199 us (0.975); the launches traced: 204 us -> 197 us
  blocking collectives: 29.8 us -> 0 us
  waiting for transfers between devices: 85.8 us -> 103 us
  starting transfers between devices: 3.67 us -> 8.12 us
  other arithmetic: 16.5 us -> 20.5 us
    all_to_all x1 -> x0, blocking collectives: 29.8 us -> none  [body(): lax.all_to_all(owned, 'chan', split_axis=1, concat_axis=2, tiled=True)]
    ppermute x0 -> x3, waiting for transfers between devices: none -> 17.2 us  [body(): lax.ppermute(sent, 'chan', [(i_2, i_2 ^ lap) for i_2 in range(size)])]
    ppermute x0 -> x3, starting transfers between devices: none -> 4.46 us  [body(): lax.ppermute(sent, 'chan', [(i_2, i_2 ^ lap) for i_2 in range(size)])]
    convert_element_type x2 -> x1, local copies, waits for them, and re-layouts: 5.93 us -> 1.81 us  [body(): grad_act.astype(jnp.float32) * gelu_slope(values)]
    unnamed x10 -> x18, local copies, waits for them, and re-layouts: 19.1 us -> 22.3 us
    convert_element_type x0 -> x1, other arithmetic: none -> 2.71 us  [body(): (grad_act.astype(jnp.float32) * gelu_slope(values)).astype(jnp.bfloat16)]
  transfers between devices with their start and end apart: 3 -> 6, of which waited for: 2 -> 4; matrix products, arithmetic and copies ran while one was open for 0% -> 1% of each run, Pallas kernels for 0% -> 0%
where the time goes in v1:
time: 199 us; the launch traced here: 197 us
  waiting for transfers between devices  103 us (52%)
  local copies, waits for them, and re-layouts  30.6 us (15%)
  matrix products  21 us (11%)
  other arithmetic  20.5 us (10%)
  between operations  13.7 us (7%)
  starting transfers between devices  8.12 us (4%)
    unnamed x2, waiting for transfers between devices  81.6 us
    unnamed x18, local copies, waits for them, and re-layouts  22.3 us
    ppermute x3, waiting for transfers between devices, body(): lax.ppermute(sent, 'chan', [(i_2, i_2 ^ lap) for i_2 in range(size)])  17.2 us
    dot_general x1, matrix products, body(): lax.dot_general(stacked, conv_weight, (((0, 1), (0, 1)), ((), ())), prefe...  17 us
    unnamed x26, other arithmetic  14.2 us
    convert_element_type x1, local copies, waits for them, and re-layouts, body(): return result.astype(jnp.bfloat16)  4.47 us
    ppermute x3, starting transfers between devices, body(): lax.ppermute(sent, 'chan', [(i_2, i_2 ^ lap) for i_2 in range(size)])  4.46 us
    ppermute x1, waiting for transfers between devices, with_halo(): lax.ppermute(head, axis, [((i + 1) % count, i) for i in range(ends)])  4.17 us
  transfers between devices with their start and end apart: 6, of which 4 were waited for; matrix products, arithmetic and copies ran while one was open for 1% of the time, Pallas kernels for 0%

profile of v1, /device:TPU:0, one launch (start us, length us, event | category | flops | bytes accessed | tf_op | source)
XLA Modules:
  0.0 196.9 jit_solution(10058135268933550500)
XLA Ops:
  6.5 2.8 %copy.107 = bf16[128,4,1024]{0,2,1:T(8,128)(2,1)} copy(bf16[128,4,1024]{2,1,0:T(4,128)(2,1)} %param.4) | data formatting | bytes 2097152 | tf_op args[0]
  9.3 1.2 fusion.89
  10.5 2.4 %collective-permute-start = (bf16[128,1,1024]{0,2,1:T(8,128)(2,1)S(1)}, bf16[128,1,1024]{0,2,1:T(8,128)(2,1)S(1)}, u32[]{:S(2)}, u32[]{:S(2)}) collective-permute-start(bf16[128,1,1024]{0,2,1:T(8,128)(2,1)S(1)} %get-tuple-element.9), channel_id=1, source_target_pairs={{0,1},{1,2},{2,3},{4,5},{5,6},{6,7},{8,9},{9,10},{10,11},{12,13},{... | collective-permute-start | bytes 786440 | tf_op jit(solution)/shard_map/ppermute | solution.py:29
  12.9 1.3 collective-permute-start.1
  14.2 4.2 %collective-permute-done.1 = bf16[128,1,1024]{0,2,1:T(8,128)(2,1)S(1)} collective-permute-done((bf16[128,1,1024]{0,2,1:T(8,128)(2,1)S(1)}, bf16[128,1,1024]{0,2,1:T(8,128)(2,1)S(1)}, u32[]{:S(2)}, u32[]{:S(2)}) %collective-permute-start.1) | collective-permute-done | bytes 262176 | tf_op jit(solution)/shard_map/ppermute | solution.py:31
  18.4 1.6 fusion.18
  33.1 0.8 fusion.24
  35.0 17.0 %bitcast_convert_fusion = bf16[4,1024,512]{2,1,0:T(8,128)(2,1)} fusion(bf16[27,128,4,1024]{1,3,0,2:T(8,128)(2,1)S(1)} %fusion.20, bf16[27,128,512]{2,1,0:T(8,128)(2,1)S(1)} %copy-done), kind=kOutput, calls=%fused_computation.1 | convolution fusion | flops 14497611776 | bytes 36044800 | tf_op jit(solution)/shard_map/dot_general | solution.py:64
  52.0 8.0 %copy.151 = bf16[4,1024,512]{1,0,2:T(4,128)(2,1)} copy(bf16[4,1024,512]{2,1,0:T(8,128)(2,1)} %bitcast_convert_fusion) | data formatting | bytes 8388608
  60.0 6.6 %copy.157 = bf16[64,8,4,1024]{3,1,2,0:T(8,128)(2,1)} copy(bf16[64,8,4,1024]{3,2,1,0:T(4,128)(2,1)} %bitcast.208) | data formatting | bytes 8388608
  66.6 81.6 %reduce-scatter.4.cloned.1.call-done = bf16[128,4096]{1,0:T(8,128)(2,1)} async-done(((bf16[512,4096]{1,0:T(8,128)(2,1)}), bf16[128,4096]{1,0:T(8,128)(2,1)}) %reduce-scatter.4.cloned.1.call-update) | async-done | bytes 1048592
  148.2 1.8 reshape.44
  150.1 1.0 copy.152
  151.2 1.6 collective-permute-start.2
  152.8 1.6 collective-permute-start.3
  154.4 1.3 collective-permute-start.4
  155.7 1.3 copy.144
  157.0 7.5 %collective-permute-done.2 = bf16[4,256,128]{2,1,0:T(8,128)(2,1)S(1)} collective-permute-done((bf16[4,256,128]{2,1,0:T(8,128)(2,1)S(1)}, bf16[4,256,128]{2,1,0:T(8,128)(2,1)S(1)}, u32[]{:S(2)}, u32[]{:S(2)}) %collective-permute-start.2) | collective-permute-done | bytes 262176 | tf_op jit(solution)/shard_map/ppermute | solution.py:75
  164.4 9.7 %collective-permute-done.3 = bf16[4,256,128]{2,1,0:T(8,128)(2,1)S(1)} collective-permute-done((bf16[4,256,128]{2,1,0:T(8,128)(2,1)S(1)}, bf16[4,256,128]{2,1,0:T(8,128)(2,1)S(1)}, u32[]{:S(2)}, u32[]{:S(2)}) %collective-permute-start.3) | collective-permute-done | bytes 262176 | tf_op jit(solution)/shard_map/ppermute | solution.py:75
  174.9 1.2 pad_maximum_fusion.2
  177.0 1.8 copy.143
  178.9 2.7 %fusion.13 = bf16[4,256,512]{1,2,0:T(8,128)(2,1)S(1)} fusion(bf16[4,256,512]{1,2,0:T(8,128)(2,1)} %copy.144, f32[4,256,4,128]{1,3,2,0:T(8,128)} %copy.143), kind=kLoop, calls=%fused_computation.21 | loop fusion | flops 5767168 | bytes 4194304 | tf_op jit(solution)/shard_map/convert_element_type | solution.py:79
  181.6 4.0 %convolution_convert_fusion = bf16[4,256,8,256]{3,1,2,0:T(8,128)(2,1)S(1)} fusion(bf16[8,256,512]{2,1,0:T(8,128)(2,1)} %param.7, bf16[4,256,512]{1,2,0:T(8,128)(2,1)S(1)} %fusion.13), kind=kOutput, calls=%fused_computation.11 | convolution fusion | flops 2149580800 | bytes 7340032 | tf_op jit(solution)/shard_map/dot_general | solution.py:80
  185.6 4.5 %copy.146 = bf16[4,256,8,256]{3,2,1,0:T(8,128)(2,1)} copy(bf16[4,256,8,256]{3,1,2,0:T(8,128)(2,1)S(1)} %convolution_convert_fusion) | data formatting | bytes 8388608 | tf_op jit(solution)/shard_map/convert_element_type | solution.py:83
  (50 shorter events, 15.8 us)
Async XLA Ops:
  6.5 28.4 %copy-start = (bf16[27,128,512]{2,1,0:T(8,128)(2,1)S(1)}, bf16[27,128,512]{2,1,0:T(8,128)(2,1)}, u32[]{:S(2)}) copy-start(bf16[27,128,512]{2,1,0:T(8,128)(2,1)} %param.5) | copy-start | bytes 10616836
  6.5 141.7 %reduce-scatter.4.cloned.1.call-start = ((), (), s32[]{:S(2)}) async-start(), calls=%async_computation.1 | async-start | bytes 5242880
  9.3 12.8 %copy-start.2 = (bf16[128,4,1024]{0,2,1:T(8,128)(2,1)S(1)}, bf16[128,4,1024]{0,2,1:T(8,128)(2,1)}, u32[]{:S(2)}) copy-start(bf16[128,4,1024]{0,2,1:T(8,128)(2,1)} %copy.107) | copy-start | bytes 3145732
  10.5 3.7 %collective-permute-start = (bf16[128,1,1024]{0,2,1:T(8,128)(2,1)S(1)}, bf16[128,1,1024]{0,2,1:T(8,128)(2,1)S(1)}, u32[]{:S(2)}, u32[]{:S(2)}) collective-permute-start(bf16[128,1,1024]{0,2,1:T(8,128)(2,1)S(1)} %get-tuple-element.9), channel_id=1, source_target_pairs={{0,1},{1,2},{2,3},{4,5},{5,6},{6,7},{8,9},{9,10},{10,11},{12,13},{... | collective-permute-start | bytes 786440 | tf_op jit(solution)/shard_map/ppermute | solution.py:29
  12.9 5.5 %collective-permute-start.1 = (bf16[128,1,1024]{0,2,1:T(8,128)(2,1)S(1)}, bf16[128,1,1024]{0,2,1:T(8,128)(2,1)S(1)}, u32[]{:S(2)}, u32[]{:S(2)}) collective-permute-start(bf16[128,1,1024]{0,2,1:T(8,128)(2,1)S(1)} %get-tuple-element.10), channel_id=1, source_target_pairs={{1,0},{2,1},{3,2},{5,4},{6,5},{7,6},{9,8},{10,9},{11,10},{13,12},{... | collective-permute-start | bytes 786440 | tf_op jit(solution)/shard_map/ppermute | solution.py:31
  60.0 95.7 %copy-start.3 = (bf16[4,256,512]{2,1,0:T(8,128)(2,1)S(1)}, bf16[4,256,512]{2,1,0:T(8,128)(2,1)}, u32[]{:S(2)}) copy-start(bf16[4,256,512]{2,1,0:T(8,128)(2,1)} %param.6) | copy-start | bytes 3145732
  151.2 13.2 %collective-permute-start.2 = (bf16[4,256,128]{2,1,0:T(8,128)(2,1)S(1)}, bf16[4,256,128]{2,1,0:T(8,128)(2,1)S(1)}, u32[]{:S(2)}, u32[]{:S(2)}) collective-permute-start(bf16[4,256,128]{2,1,0:T(8,128)(2,1)S(1)} %get-tuple-element.7), channel_id=1, source_target_pairs={{0,4},{4,0},{8,12},{12,8},{1,5},{5,1},{9,13},{13,9},{2,6},{6,2},{1... | collective-permute-start | bytes 786440 | tf_op jit(solution)/shard_map/ppermute | solution.py:75
  152.8 21.4 %collective-permute-start.3 = (bf16[4,256,128]{2,1,0:T(8,128)(2,1)S(1)}, bf16[4,256,128]{2,1,0:T(8,128)(2,1)S(1)}, u32[]{:S(2)}, u32[]{:S(2)}) collective-permute-start(bf16[4,256,128]{2,1,0:T(8,128)(2,1)S(1)} %get-tuple-element.6), channel_id=1, source_target_pairs={{0,8},{4,12},{8,0},{12,4},{1,9},{5,13},{9,1},{13,5},{2,10},{6,14},... | collective-permute-start | bytes 786440 | tf_op jit(solution)/shard_map/ppermute | solution.py:75
  154.4 19.7 %collective-permute-start.4 = (bf16[4,256,128]{2,1,0:T(8,128)(2,1)S(1)}, bf16[4,256,128]{2,1,0:T(8,128)(2,1)S(1)}, u32[]{:S(2)}, u32[]{:S(2)}) collective-permute-start(bf16[4,256,128]{2,1,0:T(8,128)(2,1)S(1)} %get-tuple-element.8), channel_id=1, source_target_pairs={{0,12},{4,8},{8,4},{12,0},{1,13},{5,9},{9,5},{13,1},{2,14},{6,10},... | collective-permute-start | bytes 786440 | tf_op jit(solution)/shard_map/ppermute | solution.py:75
  174.1 0.7 copy-start.4
  174.1 0.8 copy-start.5
  178.9 11.2 %copy-start.1 = (bf16[27,128,512]{2,1,0:T(8,128)(2,1)S(1)}, bf16[27,128,512]{2,1,0:T(8,128)(2,1)}, u32[]{:S(2)}) copy-start(bf16[27,128,512]{2,1,0:T(8,128)(2,1)} %param.5) | copy-start | bytes 10616836
Sparse Core Ops, SparseCore 0:
  66.7 81.4 reduce-scatter.3
